TPU v7x, 32 devices: a whole 2x2x4 slice. The times are simulated.
32 devices in a mesh: groups: 2 (over y), dp: 16 (over z, x, core).
Axes of the slice: x: 2, y: 2, z: 4, core: 2. Of those that a mesh axis runs over, the one named last changes fastest.
Arguments:
- state: bfloat16 [32, 128, 64, 128], P(('groups', 'dp')), parts along dimension 0, may hold values from -6 to 6
- x_in: bfloat16 [32, 8192], P(('groups', 'dp')), parts along dimension 0, may hold values from -6 to 6
- z_gate: bfloat16 [32, 8192], P(('groups', 'dp')), parts along dimension 0, may hold values from -6 to 6
- b_in: bfloat16 [32, 512], P(('groups', 'dp')), parts along dimension 0, may hold values from -6 to 6
- c_in: bfloat16 [32, 512], P(('groups', 'dp')), parts along dimension 0, may hold values from -0.59765625 to 0.59765625
- dt_raw: float32 [32, 128], P(('groups', 'dp')), parts along dimension 0, may hold values from -5 to 5
- dt_bias: float32 [128], replicated, may hold values from -3 to 0.5
- a_log: float32 [128], replicated, may hold values from -1 to 1.5
- d_skip: float32 [128], replicated, may hold values from 0.3 to 1.7
- norm_gain: float32 [8192], replicated, may hold values from 0.1 to 1.9
- out_proj: bfloat16 [8192, 8192], P('dp'), may hold values from -0.0625 to 0.0625
- active: int32 [32], P(('groups', 'dp')), parts along dimension 0, may hold values from 0 to 1
- plan: int32 [16, 2], P('groups'), parts along dimension 0, may hold values from 0 to 15, as said below
Outputs:
- mixed: bfloat16 [32, 8192], P(('groups', 'dp')), parts along dimension 0
- new_state: bfloat16 [32, 128, 64, 128], P(('groups', 'dp')), parts along dimension 0
There are 2 independent parts, one for each index of `groups`. A program takes and returns all parts, laid end to end along the dimension named above; an argument that names none is the same for every part. Nothing has to cross between parts.
Inputs may be any that keep to these rules, and one draw needn't show every extreme that they name: `plan`: exactly 8 moves. Source slots are distinct and live in active; destination slots are distinct and not live in active. Slot k belongs to device k. Each device holds the source of at most one move and the destination of at most one, never both; both bounds are reached.
All inputs are finite; a program needn't handle non-finite values.
Results may differ from a plain program's by a relative error of at most 0.0049.
Values may be sent and summed in bfloat16 or wider, within the bound.
No kernel may reach another device: no remote copies, remote signals or barrier semaphores. Data moves between devices by JAX's collectives and lax.ppermute only.
A program may use at most 64 MiB of HBM per device.

v0:
```python
import functools

import jax
import jax.numpy as jnp
from jax import lax
from jax.experimental import pallas as pl
from jax.experimental.pallas import tpu as pltpu
from jax.sharding import PartitionSpec as P

AXIS = "dp"
LANES = 128
MOST_PATTERNS = 32
TILE = 1024
FIRST = 2
GRANT = 16 * 2**20
F32 = jnp.float32
BF16 = jnp.bfloat16


def pair_switch(index, devices, state, rows_of, beside, operands):
    def branch(distance, low_sends):
        pairs = [(i, i ^ distance) for i in range(devices) if (i < (i ^ distance)) == low_sends]
        back = [(t, s) for s, t in pairs]

        def move(state, operands):
            came = lax.ppermute(state, AXIS, pairs)
            theirs = lax.ppermute(rows_of(*operands), AXIS, back)
            return came, beside(theirs, state, *operands)

        return move

    branches = [branch(d, low) for d in range(1, devices) for low in (True, False)]
    return lax.switch(index, branches, state, operands)


def index_kernel(me, plan, index, live):
    def move(k, found):
        partner, sends = found
        source, target = plan[0, k], plan[1, k]
        partner = jnp.where(source == me[0], target, jnp.where(target == me[0], source, partner))
        return partner, jnp.where(source == me[0], 1, sends)

    partner, sends = lax.fori_loop(0, plan.shape[1], move, (jnp.int32(0), jnp.int32(0)))
    low_sends = jnp.where(me[0] < partner, sends, 1 - sends)
    index[0] = 2 * (jnp.bitwise_xor(me[0], partner) - 1) + 1 - low_sends
    live[0] = 1 - sends


def spread_and_collect(state, source, target, devices):
    ids = jnp.arange(devices, dtype=jnp.int32)
    matches = target[:, None] == ids[None, :]
    sender_of = jnp.sum(jnp.where(matches, source[:, None], 0), axis=0)
    has_sender = jnp.any(matches, axis=0)
    view = lax.all_to_all(state, AXIS, split_axis=1, concat_axis=0, tiled=True)
    routed = jnp.where(
        has_sender[:, None, None, None], jnp.take(view, sender_of, axis=0), jnp.zeros((), state.dtype)
    )
    return lax.all_to_all(routed, AXIS, split_axis=0, concat_axis=1, tiled=True)


def split(value):
    first = value.astype(BF16).astype(F32)
    second = (value - first).astype(BF16).astype(F32)
    return first, second, value - first - second


def pack_kernel(x, z, b, c, dt, out):
    first, second, third = split(dt[...])
    upper = [x[...].astype(F32), b[...].astype(F32), first, second]
    lower = [z[...].astype(F32), c[...].astype(F32), third, jnp.zeros_like(third)]
    at = 0
    for up, low in zip(upper, lower):
        width = up.shape[1]
        shape = (2, width)
        row = lax.broadcasted_iota(jnp.int32, shape, 0)
        both = jnp.where(row == 0, jnp.broadcast_to(up, shape), jnp.broadcast_to(low, shape))
        out[:, at : at + width] = both.astype(BF16)
        at += width


def mix_kernel(s, xz, bc, per_head, gain, out):
    heads, p_size, n = s.shape
    rows = bc[...].astype(F32)
    b, c = rows[0:1], rows[1:2]
    t = lax.dot_general(
        jnp.broadcast_to(c, (16, n)).astype(BF16),
        s[...].reshape(heads * p_size, n),
        (((1,), (1,)), ((), ())),
        preferred_element_type=F32,
    )[0:1]
    both = xz[...].astype(F32)
    x, z = both[0:1], both[1:2]
    y = (
        per_head[0:1] * t
        + (per_head[1:2] * x) * jnp.sum(b * c, axis=1, keepdims=True)
        + per_head[2:3] * x
    )
    gated = y * jax.nn.silu(z)
    factor = lax.rsqrt(jnp.mean(gated * gated, axis=1, keepdims=True) + 1e-05)
    normed = (gated * factor * gain[...]).astype(BF16)
    for q in range(normed.shape[1] // LANES):
        out[q : q + 1, :] = normed[:, q * LANES : (q + 1) * LANES]


def hold_kernel(moves, w, out, takes, sem):
    copy = pltpu.make_async_copy(w.at[:, pl.ds(0, out.shape[1])], out, sem)
    copy.start()
    to = lax.broadcasted_iota(jnp.int32, takes.shape, 0)
    of = lax.broadcasted_iota(jnp.int32, takes.shape, 1)

    def add(k, found):
        return jnp.where((of == moves[0, k]) & (to == moves[1, k]), 1.0, found)

    found = lax.fori_loop(0, moves.shape[1], add, jnp.zeros(takes.shape, F32))
    takes[...] = found.astype(BF16)
    copy.wait()


def update_kernel(live, decay, s, x, b, step, out):
    heads, p_size, n = out.shape
    g = pl.program_id(0)
    dx = step[...] * x[...].astype(F32)
    first, second, third = split(dx)
    row = lax.broadcasted_iota(jnp.int32, (16, dx.shape[1]), 0)
    terms = jnp.where(
        row == 0, first, jnp.where(row == 1, second, jnp.where(row == 2, third, 0.0))
    ).astype(BF16)
    outer = lax.dot_general(
        terms, jnp.broadcast_to(b[...], (16, n)), (((0,), (0,)), ((), ())), preferred_element_type=F32
    )
    for h in range(heads):
        fresh = decay[g * heads + h] * s[h].astype(F32) + outer[h * p_size : (h + 1) * p_size]
        out[h] = jnp.where(live[0] > 0, fresh, 0.0).astype(BF16)


def project_kernel(takes, rows, first_w, w, out, rest_w, sems):
    tiles = w.shape[1] // TILE
    have = first_w.shape[1] // TILE
    copies = [
        pltpu.make_async_copy(
            w.at[:, pl.ds((have + i) * TILE, TILE)], rest_w.at[:, pl.ds(i * TILE, TILE)], sems.at[i]
        )
        for i in range(tiles - have)
    ]
    for copy in copies:
        copy.start()
    lhs = jnp.concatenate([rows[:, r, :] for r in range(rows.shape[1])], axis=1)
    lhs = jnp.dot(takes[...], lhs, preferred_element_type=F32).astype(BF16)
    for i in range(tiles):
        if i < have:
            weights = first_w[:, i * TILE : (i + 1) * TILE]
        else:
            copies[i - have].wait()
            weights = rest_w[:, (i - have) * TILE : (i - have + 1) * TILE]
        total = jnp.dot(lhs, weights, preferred_element_type=F32).astype(out.dtype)
        for j in range(TILE // LANES):
            out[:, i * (TILE // LANES) + j, :] = total[:, j * LANES : (j + 1) * LANES]


def sum_kernel(parts, out):
    total = jnp.sum(parts[...].astype(F32), axis=0).astype(BF16)
    for q in range(total.shape[0]):
        out[0:1, q * LANES : (q + 1) * LANES] = total[q : q + 1, :]


def local(
    state,
    x_in,
    z_gate,
    b_in,
    c_in,
    dt_raw,
    dt_bias,
    a_log,
    d_skip,
    norm_gain,
    out_proj,
    active,
    plan,
):
    devices = lax.axis_size(AXIS)
    me = lax.axis_index(AXIS)
    heads, p_size, n = state.shape[1:]
    groups = b_in.shape[1] // n
    width = heads * p_size
    columns = out_proj.shape[1]
    source, target = plan[:, 0], plan[:, 1]
    smem = pl.BlockSpec(memory_space=pltpu.SMEM)
    index, live = pl.pallas_call(
        index_kernel,
        name="index",
        in_specs=[smem, smem],
        out_specs=(smem, smem),
        out_shape=(pltpu.SMEM((1,), jnp.int32),) * 2,
    )(me.astype(jnp.int32).reshape(1), plan.T)

    of_group = width // groups
    vmem = pl.BlockSpec(memory_space=pltpu.VMEM)
    hbm = pl.BlockSpec(memory_space=pltpu.HBM)
    in_vmem = functools.partial(pltpu.with_memory_space_constraint, memory_space=pltpu.VMEM)
    params = pltpu.CompilerParams(vmem_limit_bytes=GRANT)
    state_spec = pl.BlockSpec((heads // groups, p_size, n), lambda g: (g, 0, 0))
    row_spec = pl.BlockSpec((1, of_group), lambda g: (0, g))
    weights = pltpu.with_memory_space_constraint(out_proj, pltpu.HBM)
    gain = norm_gain.reshape(1, width)

    def rows_of(x_in, z_gate, b_in, c_in, dt_raw, *_):
        return pl.pallas_call(
            pack_kernel,
            name="pack",
            out_shape=jax.ShapeDtypeStruct((2, width + groups * n + 2 * heads), BF16),
            compiler_params=params,
        )(x_in, z_gate, b_in, c_in, dt_raw)

    def beside(
        theirs, state, x_in, z_gate, b_in, c_in, dt_raw, dt_bias, a_log, d_skip, gain, weights, moves
    ):
        ends = theirs[:, width + groups * n :].astype(F32)
        their_dt = (ends[0, :heads] + ends[0, heads:]) + ends[1, :heads]
        step = jax.nn.softplus(jnp.stack([their_dt, dt_raw[0]]) + dt_bias)
        decay = jnp.exp(-jnp.exp(a_log) * step)
        each = jnp.stack([decay[0], step[0], d_skip, step[1]])
        per_head = jnp.repeat(each, p_size, axis=1)
        normed = pl.pallas_call(
            mix_kernel,
            name="mix",
            grid=(groups,),
            in_specs=[
                state_spec,
                pl.BlockSpec((2, of_group), lambda g: (0, g)),
                pl.BlockSpec((2, n), lambda g: (0, width // n + g)),
                pl.BlockSpec((4, of_group), lambda g: (0, g)),
                row_spec,
            ],
            out_specs=pl.BlockSpec((of_group // LANES, LANES), lambda g: (g, 0)),
            out_shape=jax.ShapeDtypeStruct((width // LANES, LANES), BF16),
            compiler_params=params,
        )(state.reshape(heads, p_size, n), theirs, theirs, per_head, gain)
        first_w, takes = pl.pallas_call(
            hold_kernel,
            name="hold",
            in_specs=[smem, hbm],
            out_specs=(vmem, vmem),
            out_shape=(
                pltpu.VMEM((weights.shape[0], FIRST * TILE), BF16),
                pltpu.VMEM((devices, devices), BF16),
            ),
            scratch_shapes=[pltpu.SemaphoreType.DMA],
            compiler_params=params,
        )(moves, pltpu.with_memory_space_constraint(weights, pltpu.HBM))
        return normed, first_w, takes, decay[1], per_head[3:4]

    operands = (x_in, z_gate, b_in, c_in, dt_raw, dt_bias, a_log, d_skip, gain, out_proj)
    if 2 * (devices - 1) <= MOST_PATTERNS and devices & (devices - 1) == 0:
        came, (normed, first_w, takes, decay, step) = pair_switch(
            index[0], devices, state, rows_of, beside, operands + (plan.T,)
        )
    else:
        came = spread_and_collect(state, source, target, devices)
        own = jnp.stack([target, target])
        normed, first_w, takes, decay, step = beside(rows_of(*operands), came, *operands, own)
    came = came.reshape(heads, p_size, n)

    block = width // devices
    lanes = min(block, LANES)
    mine = lax.all_to_all(
        normed.reshape(devices, block // lanes, lanes), AXIS, split_axis=0, concat_axis=0, tiled=True
    )

    new_state = pl.pallas_call(
        update_kernel,
        name="update",
        grid=(groups,),
        in_specs=[smem, smem, state_spec, row_spec, pl.BlockSpec((1, n), lambda g: (0, g)), row_spec],
        out_specs=state_spec,
        out_shape=jax.ShapeDtypeStruct((heads, p_size, n), BF16),
        compiler_params=params,
    )(live, decay, came, x_in, b_in, step)

    partial = pl.pallas_call(
        project_kernel,
        name="project",
        in_specs=[vmem, vmem, vmem, hbm],
        out_specs=vmem,
        out_shape=jax.ShapeDtypeStruct((devices, columns // LANES, LANES), BF16),
        scratch_shapes=[
            pltpu.VMEM((out_proj.shape[0], columns - FIRST * TILE), BF16),
            pltpu.SemaphoreType.DMA((columns // TILE - FIRST,)),
        ],
        compiler_params=params,
    )(in_vmem(takes), in_vmem(mine), in_vmem(first_w), weights)
    partial = lax.all_to_all(partial, AXIS, split_axis=0, concat_axis=0, tiled=True)
    mixed = pl.pallas_call(
        sum_kernel,
        name="total",
        in_specs=[vmem],
        out_shape=jax.ShapeDtypeStruct((1, columns), BF16),
        compiler_params=params,
    )(in_vmem(partial))
    return (mixed, new_state[None])


def solution(mesh):
    in_specs = (
        P(("groups", "dp"), None, None, None),
        P(("groups", "dp"), None),
        P(("groups", "dp"), None),
        P(("groups", "dp"), None),
        P(("groups", "dp"), None),
        P(("groups", "dp"), None),
        P(),
        P(),
        P(),
        P(),
        P("dp", None),
        P(("groups", "dp")),
        P("groups", None),
    )
    out_specs = (P(("groups", "dp"), None), P(("groups", "dp"), None, None, None))
    return jax.shard_map(local, mesh=mesh, in_specs=in_specs, out_specs=out_specs, check_vma=False)
```

profile of v0, /device:TPU:5, one launch (start us, length us, event | category | flops | bytes accessed | tf_op | source)
XLA Modules:
  0.0 102.5 jit_solution(17276211494697085411)
XLA Ops:
  0.6 0.8 index.1
  1.4 30.1 %conditional.1 = (bf16[64,128]{1,0:T(8,128)(2,1)S(1)}, bf16[512,2048]{1,0:T(8,128)(2,1)S(1)}, bf16[16,16]{1,0:T(8,128)(2,1)S(1)}, f32[128]{0:T(128)S(1)}, f32[1,...) conditional(s32[]{:T(128)} %bitcast.152, (bf16[1,128,64,128]{3,2,1,0:T(8,128)(2,1)}, ...), branch_computations={%region_0.1_spmd, %region_1.2_spmd, %region_2.3_spmd, %region_3.4_... | conditional | flops 4736 | bytes 9182448 | solution.py:33
  1.6 7.5 %collective-permute-start.53 = (bf16[1,128,64,128]{3,2,1,0:T(8,128)(2,1)}, bf16[1,128,64,128]{3,2,1,0:T(8,128)(2,1)}, u32[]{:S(2)}, u32[]{:S(2)}) collective-permute-start(bf16[1,128,64,128]{3,2,1,0:T(8,128)(2,1)} %get-tuple-element.1085), channel_id=1, source_target_pairs={{0,14},{1,15},{2,12},{3,13},{4,10},{5,11},{6,8},{7,9},{16,30},{17,... | collective-permute-start | bytes 6291464 | tf_op jit(solution)/shard_map/cond/branch_26_fun/ppermute | solution.py:26
  9.2 0.9 pack.56
  10.0 1.3 %collective-permute-start.52 = (bf16[2,8960]{1,0:T(2,128)(2,1)S(1)}, bf16[2,8960]{1,0:T(2,128)(2,1)S(1)}, u32[]{:S(2)}, u32[]{:S(2)}) collective-permute-start(bf16[2,8960]{1,0:T(2,128)(2,1)S(1)} %pack.56), channel_id=1, source_target_pairs={{14,0},{15,1},{12,2},{13,3},{10,4},{11,5},{8,6},{9,7},{30,16},{31,... | collective-permute-start | bytes 107528 | tf_op jit(solution)/shard_map/cond/branch_26_fun/ppermute | solution.py:27
  11.3 0.7 exponential_negate_fusion.26
  12.0 0.0 copy-start.58
  12.0 0.0 copy-start.88
  12.0 0.0 copy-start.118
  12.0 0.0 copy-start.27
  12.0 2.4 %hold.56 = (bf16[512,2048]{1,0:T(8,128)(2,1)S(1)}, bf16[16,16]{1,0:T(8,128)(2,1)S(1)}) custom-call(s32[2,8]{1,0:T(2,128)} %get-tuple-element.1095.moves, bf16[512,8192]{1,0:T(8,128)(2,1)} %get-tuple-element.1096.w), custom_call_target="tpu_custom_call" | custom-call | tf_op jit(solution)/shard_map/cond/branch_26_fun/hold/pallas_call | solution.py:239
  14.4 3.4 %collective-permute-done.52.xz.bc = bf16[2,8960]{1,0:T(2,128)(2,1)S(1)} collective-permute-done((bf16[2,8960]{1,0:T(2,128)(2,1)S(1)}, bf16[2,8960]{1,0:T(2,128)(2,1)S(1)}, u32[]{:S(2)}, u32[]{:S(2)}) %collective-permute-start.52) | collective-permute-done | bytes 35872 | tf_op jit(solution)/shard_map/cond/branch_26_fun/ppermute | solution.py:27
  17.8 0.0 copy-done.58
  17.8 0.0 copy-done.88
  17.9 0.1 broadcast_in_dim.261
  17.9 0.1 broadcast_in_dim.262
  18.1 0.0 copy-done.118
  18.1 0.1 broadcast_in_dim.260
  18.2 0.1 reshape.453.per_head
  18.4 0.0 copy-done.27
  18.4 3.3 %mix.56 = bf16[64,128]{1,0:T(8,128)(2,1)S(1)} custom-call(bf16[128,64,128]{2,1,0:T(8,128)(2,1)} %bitcast.242, bf16[2,8960]{1,0:T(2,128)(2,1)S(1)} %collective-permute-done.52.xz.bc, bf16[2,8960]{1,0:T(2,128)(2,1)S(1)} %collective-permute-done.52.xz.bc, f32[4,8192]{1,0:T(4,128)S(1)} %reshape.453.per_head, f32[1,8192]{1,0:T(1,128)S(1)} %copy-done.27), custom_call_target="tpu_custom_call" | custom-call | tf_op jit(solution)/shard_map/cond/branch_26_fun/mix/pallas_call | solution.py:224
  21.7 9.8 %collective-permute-done.53 = bf16[1,128,64,128]{3,2,1,0:T(8,128)(2,1)} collective-permute-done((bf16[1,128,64,128]{3,2,1,0:T(8,128)(2,1)}, bf16[1,128,64,128]{3,2,1,0:T(8,128)(2,1)}, u32[]{:S(2)}, u32[]{:S(2)}) %collective-permute-start.53) | collective-permute-done | bytes 2097184 | tf_op jit(solution)/shard_map/cond/branch_26_fun/ppermute | solution.py:26
  31.5 52.7 %all_to_all.10.rows = bf16[16,4,128]{2,1,0:T(4,128)(2,1)S(1)} all-to-all(bf16[16,4,128]{2,1,0:T(4,128)(2,1)S(1)} %bitcast.338), channel_id=1, replica_groups=mesh['groups'=2,'dp'=16] {'dp'}, dimensions={0} | all-to-all | bytes 32768 | tf_op jit(solution)/shard_map/all_to_all | solution.py:266
  84.2 0.0 copy-start
  84.2 0.0 copy-start.31
  84.2 3.9 %project.1 = bf16[16,64,128]{2,1,0:T(8,128)(2,1)} custom-call(bf16[16,16]{1,0:T(8,128)(2,1)S(1)} %get-tuple-element.1152.takes, bf16[16,4,128]{2,1,0:T(4,128)(2,1)S(1)} %all_to_all.10.rows, bf16[512,2048]{1,0:T(8,128)(2,1)S(1)} %get-tuple-element.1154.first_w, bf16[512,8192]{1,0:T(8,128)(2,1)} %w.1), custom_call_target="tpu_custom_call" | custom-call | tf_op jit(solution)/shard_map/project/pallas_call | solution.py:280
  88.1 4.1 %all-to-all-start.1 = ((bf16[16,64,128]{2,1,0:T(8,128)(2,1)}), bf16[16,64,128]{2,1,0:T(8,128)(2,1)S(1)}, u32[]{:S(2)}, u32[]{:S(2)}) async-start(bf16[16,64,128]{2,1,0:T(8,128)(2,1)} %project.1), calls=%async_computation.1 | async-start | bytes 524288 | tf_op jit(solution)/shard_map/all_to_all | solution.py:292
  92.2 0.0 copy-done
  92.2 0.0 copy-done.31
  92.2 4.5 %update.1 = bf16[128,64,128]{2,1,0:T(8,128)(2,1)} custom-call(s32[1]{0:T(128)S(4)} %get-tuple-element.1155.live, f32[128]{0:T(128)S(1)} %get-tuple-element.1156.decay, bf16[128,64,128]{2,1,0:T(8,128)(2,1)} %get-tuple-element.1157.s, bf16[1,8192]{1,0:T(2,128)(2,1)S(1)} %copy-done, bf16[1,512]{1,0:T(2,128)(2,1)S(1)} %copy-done.31, ...), custom_call_target="tpu_custom_call" | custom-call | tf_op jit(solution)/shard_map/update/pallas_call | solution.py:270
  96.7 5.1 %all-to-all-done.1.parts = bf16[16,64,128]{2,1,0:T(8,128)(2,1)S(1)} async-done(((bf16[16,64,128]{2,1,0:T(8,128)(2,1)}), bf16[16,64,128]{2,1,0:T(8,128)(2,1)S(1)}, u32[]{:S(2)}, u32[]{:S(2)}) %all-to-all-start.1) | async-done | bytes 262176 | tf_op jit(solution)/shard_map/all_to_all | solution.py:292
  101.8 0.7 total.1
  (6 shorter events, 0.1 us)
Async XLA Ops:
  1.6 29.9 %collective-permute-start.53 = (bf16[1,128,64,128]{3,2,1,0:T(8,128)(2,1)}, bf16[1,128,64,128]{3,2,1,0:T(8,128)(2,1)}, u32[]{:S(2)}, u32[]{:S(2)}) collective-permute-start(bf16[1,128,64,128]{3,2,1,0:T(8,128)(2,1)} %get-tuple-element.1085), channel_id=1, source_target_pairs={{0,14},{1,15},{2,12},{3,13},{4,10},{5,11},{6,8},{7,9},{16,30},{17,... | collective-permute-start | bytes 6291464 | tf_op jit(solution)/shard_map/cond/branch_26_fun/ppermute | solution.py:26
  10.0 7.8 %collective-permute-start.52 = (bf16[2,8960]{1,0:T(2,128)(2,1)S(1)}, bf16[2,8960]{1,0:T(2,128)(2,1)S(1)}, u32[]{:S(2)}, u32[]{:S(2)}) collective-permute-start(bf16[2,8960]{1,0:T(2,128)(2,1)S(1)} %pack.56), channel_id=1, source_target_pairs={{14,0},{15,1},{12,2},{13,3},{10,4},{11,5},{8,6},{9,7},{30,16},{31,... | collective-permute-start | bytes 107528 | tf_op jit(solution)/shard_map/cond/branch_26_fun/ppermute | solution.py:27
  12.0 5.8 %copy-start.58 = (f32[1,128]{1,0:T(1,128)S(1)}, f32[1,128]{1,0:T(1,128)}, u32[]{:S(2)}) copy-start(f32[1,128]{1,0:T(1,128)} %get-tuple-element.1090.dt) | copy-start | bytes 1540 | tf_op jit(solution)/shard_map/cond
  12.0 5.8 %copy-start.88 = (f32[128]{0:T(128)S(1)}, f32[128]{0:T(128)}, u32[]{:S(2)}) copy-start(f32[128]{0:T(128)} %get-tuple-element.1092) | copy-start | bytes 1540 | tf_op jit(solution)/shard_map/cond
  12.0 6.1 %copy-start.118 = (f32[128]{0:T(128)S(1)}, f32[128]{0:T(128)}, u32[]{:S(2)}) copy-start(f32[128]{0:T(128)} %get-tuple-element.1093) | copy-start | bytes 1540 | tf_op jit(solution)/shard_map/cond
  12.0 6.4 %copy-start.27 = (f32[1,8192]{1,0:T(1,128)S(1)}, f32[1,8192]{1,0:T(1,128)}, u32[]{:S(2)}) copy-start(f32[1,8192]{1,0:T(1,128)} %get-tuple-element.1094.gain) | copy-start | bytes 98308 | tf_op jit(solution)/shard_map/cond
  84.2 8.0 %copy-start = (bf16[1,8192]{1,0:T(2,128)(2,1)S(1)}, bf16[1,8192]{1,0:T(2,128)(2,1)}, u32[]{:S(2)}) copy-start(bf16[1,8192]{1,0:T(2,128)(2,1)} %x.1) | copy-start | bytes 49156
  84.2 8.0 %copy-start.31 = (bf16[1,512]{1,0:T(2,128)(2,1)S(1)}, bf16[1,512]{1,0:T(2,128)(2,1)}, u32[]{:S(2)}) copy-start(bf16[1,512]{1,0:T(2,128)(2,1)} %b.1) | copy-start | bytes 3076
  88.1 13.7 %all-to-all-start.1 = ((bf16[16,64,128]{2,1,0:T(8,128)(2,1)}), bf16[16,64,128]{2,1,0:T(8,128)(2,1)S(1)}, u32[]{:S(2)}, u32[]{:S(2)}) async-start(bf16[16,64,128]{2,1,0:T(8,128)(2,1)} %project.1), calls=%async_computation.1 | async-start | bytes 524288 | tf_op jit(solution)/shard_map/all_to_all | solution.py:292
where the time goes:
time: 105 us; the launch traced here: 102 us
  blocking collectives  52.7 us (50%)
  waiting for transfers between devices  18.3 us (17%)
  Pallas kernels  16.4 us (16%)
  starting transfers between devices  12.9 us (12%)
    all_to_all x1, blocking collectives, local(): lax.all_to_all(normed.reshape(devices, block // lanes, lanes), AXIS, spli...  52.7 us
    ppermute x1, waiting for transfers between devices, move(): came = lax.ppermute(state, AXIS, pairs)  9.85 us
    ppermute x1, starting transfers between devices, move(): came = lax.ppermute(state, AXIS, pairs)  7.52 us
    all_to_all x1, waiting for transfers between devices, local(): lax.all_to_all(partial, AXIS, split_axis=0, concat_axis=0, tiled=True)  5.09 us
    pallas_call x1, Pallas kernels, local(): pl.pallas_call(update_kernel, name='update', grid=(groups,), in_specs=[sm...  4.47 us
    all_to_all x1, starting transfers between devices, local(): lax.all_to_all(partial, AXIS, split_axis=0, concat_axis=0, tiled=True)  4.09 us
    pallas_call x1, Pallas kernels, local(): pl.pallas_call(project_kernel, name='project', in_specs=[vmem, vmem, vmem...  3.91 us
    ppermute x1, waiting for transfers between devices, move(): theirs = lax.ppermute(rows_of(*operands), AXIS, back)  3.36 us
  transfers between devices with their start and end apart: 3, of which 3 were waited for; matrix products, arithmetic and copies ran while one was open for 1% of the time, Pallas kernels for 11%

commit v1 on v0

--- a/solution.py
+++ b/solution.py
@@ -11,7 +11,7 @@
 LANES = 128
 MOST_PATTERNS = 32
 TILE = 1024
-FIRST = 2
+FIRST = 3
 GRANT = 16 * 2**20
 F32 = jnp.float32
 BF16 = jnp.bfloat16

time: 105 us -> 105 us (level)
  the two profiles are of different devices: /device:TPU:5 before, /device:TPU:0 now
where the time goes in v1:
time: 105 us; the launch traced here: 104 us
  blocking collectives  53.9 us (51%)
  waiting for transfers between devices  17.5 us (17%)
  Pallas kernels  16.4 us (16%)
  starting transfers between devices  12.1 us (12%)
  local copies, waits for them, and re-layouts  2.14 us (2%)
    all_to_all x1, blocking collectives, local(): lax.all_to_all(normed.reshape(devices, block // lanes, lanes), AXIS, spli...  53.9 us
    ppermute x1, waiting for transfers between devices, move(): came = lax.ppermute(state, AXIS, pairs)  12 us
    ppermute x1, starting transfers between devices, move(): theirs = lax.ppermute(rows_of(*operands), AXIS, back)  7.24 us
    all_to_all x1, waiting for transfers between devices, local(): lax.all_to_all(partial, AXIS, split_axis=0, concat_axis=0, tiled=True)  5.49 us
    pallas_call x1, Pallas kernels, local(): pl.pallas_call(update_kernel, name='update', grid=(groups,), in_specs=[sm...  4.47 us
    pallas_call x1, Pallas kernels, local(): pl.pallas_call(project_kernel, name='project', in_specs=[vmem, vmem, vmem...  3.58 us
    all_to_all x1, starting transfers between devices, local(): lax.all_to_all(partial, AXIS, split_axis=0, concat_axis=0, tiled=True)  3.54 us
    pallas_call x1, Pallas kernels, beside(): pl.pallas_call(mix_kernel, name='mix', grid=(groups,), in_specs=[state_sp...  3.28 us
  transfers between devices with their start and end apart: 3, of which 2 were waited for; matrix products, arithmetic and copies ran while one was open for 3% of the time, Pallas kernels for 11%

profile of v1, /device:TPU:0, one launch (start us, length us, event | category | flops | bytes accessed | tf_op | source)
XLA Modules:
  0.0 103.6 jit_solution(3685539239868455249)
XLA Ops:
  0.6 0.8 index.1
  1.4 30.4 %conditional.1 = (bf16[64,128]{1,0:T(8,128)(2,1)S(1)}, bf16[512,3072]{1,0:T(8,128)(2,1)S(1)}, bf16[16,16]{1,0:T(8,128)(2,1)S(1)}, f32[128]{0:T(128)S(1)}, f32[1,...) conditional(s32[]{:T(128)} %bitcast.152, (bf16[1,128,64,128]{3,2,1,0:T(8,128)(2,1)}, ...), branch_computations={%region_0.1_spmd, %region_1.2_spmd, %region_2.3_spmd, %region_3.4_... | conditional | flops 4736 | bytes 9182448 | solution.py:33
  1.4 1.3 %collective-permute-start.23 = (bf16[1,128,64,128]{3,2,1,0:T(8,128)(2,1)}, bf16[1,128,64,128]{3,2,1,0:T(8,128)(2,1)}, u32[]{:S(2)}, u32[]{:S(2)}) collective-permute-start(bf16[1,128,64,128]{3,2,1,0:T(8,128)(2,1)} %get-tuple-element.875), channel_id=1, source_target_pairs={{4,2},{5,3},{6,0},{7,1},{12,10},{13,11},{14,8},{15,9},{20,18},{21,... | collective-permute-start | bytes 6291464 | tf_op jit(solution)/shard_map/cond/branch_11_fun/ppermute | solution.py:26
  2.7 0.9 pack.41
  3.6 7.2 %collective-permute-start.22 = (bf16[2,8960]{1,0:T(2,128)(2,1)S(1)}, bf16[2,8960]{1,0:T(2,128)(2,1)S(1)}, u32[]{:S(2)}, u32[]{:S(2)}) collective-permute-start(bf16[2,8960]{1,0:T(2,128)(2,1)S(1)} %pack.41), channel_id=1, source_target_pairs={{2,4},{3,5},{0,6},{1,7},{10,12},{11,13},{8,14},{9,15},{18,20},{19,... | collective-permute-start | bytes 107528 | tf_op jit(solution)/shard_map/cond/branch_11_fun/ppermute | solution.py:27
  10.9 0.7 exponential_negate_fusion.11
  11.5 0.0 copy-start.43
  11.5 0.0 copy-start.73
  11.5 0.0 copy-start.103
  11.5 0.0 copy-start.12
  11.5 2.7 %hold.41 = (bf16[512,3072]{1,0:T(8,128)(2,1)S(1)}, bf16[16,16]{1,0:T(8,128)(2,1)S(1)}) custom-call(s32[2,8]{1,0:T(2,128)} %get-tuple-element.885.moves, bf16[512,8192]{1,0:T(8,128)(2,1)} %get-tuple-element.886.w), custom_call_target="tpu_custom_call" | custom-call | tf_op jit(solution)/shard_map/cond/branch_11_fun/hold/pallas_call | solution.py:239
  14.3 0.0 collective-permute-done.22.xz.bc
  14.3 0.0 copy-done.43
  14.3 0.0 copy-done.73
  14.4 0.1 broadcast_in_dim.216
  14.4 0.1 broadcast_in_dim.217
  14.6 0.0 copy-done.103
  14.6 0.8 broadcast_in_dim.215
  15.4 1.1 %reshape.408.per_head = f32[4,8192]{1,0:T(4,128)S(1)} reshape(f32[4,128,64]{2,1,0:T(8,128)} %broadcast_in_dim.215) | data formatting | bytes 262144 | tf_op jit(solution)/shard_map/cond/branch_11_fun/reshape | solution.py:223
  16.5 0.0 copy-done.12
  16.5 3.3 %mix.41 = bf16[64,128]{1,0:T(8,128)(2,1)S(1)} custom-call(bf16[128,64,128]{2,1,0:T(8,128)(2,1)} %bitcast.227, bf16[2,8960]{1,0:T(2,128)(2,1)S(1)} %collective-permute-done.22.xz.bc, bf16[2,8960]{1,0:T(2,128)(2,1)S(1)} %collective-permute-done.22.xz.bc, f32[4,8192]{1,0:T(4,128)S(1)} %reshape.408.per_head, f32[1,8192]{1,0:T(1,128)S(1)} %copy-done.12), custom_call_target="tpu_custom_call" | custom-call | tf_op jit(solution)/shard_map/cond/branch_11_fun/mix/pallas_call | solution.py:224
  19.8 12.0 %collective-permute-done.23 = bf16[1,128,64,128]{3,2,1,0:T(8,128)(2,1)} collective-permute-done((bf16[1,128,64,128]{3,2,1,0:T(8,128)(2,1)}, bf16[1,128,64,128]{3,2,1,0:T(8,128)(2,1)}, u32[]{:S(2)}, u32[]{:S(2)}) %collective-permute-start.23) | collective-permute-done | bytes 2097184 | tf_op jit(solution)/shard_map/cond/branch_11_fun/ppermute | solution.py:26
  31.8 53.9 %all_to_all.10.rows = bf16[16,4,128]{2,1,0:T(4,128)(2,1)S(1)} all-to-all(bf16[16,4,128]{2,1,0:T(4,128)(2,1)S(1)} %bitcast.338), channel_id=1, replica_groups=mesh['groups'=2,'dp'=16] {'dp'}, dimensions={0} | all-to-all | bytes 32768 | tf_op jit(solution)/shard_map/all_to_all | solution.py:266
  85.8 0.0 copy-start
  85.8 0.0 copy-start.31
  85.8 3.6 %project.1 = bf16[16,64,128]{2,1,0:T(8,128)(2,1)} custom-call(bf16[16,16]{1,0:T(8,128)(2,1)S(1)} %get-tuple-element.1152.takes, bf16[16,4,128]{2,1,0:T(4,128)(2,1)S(1)} %all_to_all.10.rows, bf16[512,3072]{1,0:T(8,128)(2,1)S(1)} %get-tuple-element.1154.first_w, bf16[512,8192]{1,0:T(8,128)(2,1)} %w.1), custom_call_target="tpu_custom_call" | custom-call | tf_op jit(solution)/shard_map/project/pallas_call | solution.py:280
  89.3 3.5 %all-to-all-start.1 = ((bf16[16,64,128]{2,1,0:T(8,128)(2,1)}), bf16[16,64,128]{2,1,0:T(8,128)(2,1)S(1)}, u32[]{:S(2)}, u32[]{:S(2)}) async-start(bf16[16,64,128]{2,1,0:T(8,128)(2,1)} %project.1), calls=%async_computation.1 | async-start | bytes 524288 | tf_op jit(solution)/shard_map/all_to_all | solution.py:292
  92.9 0.0 copy-done
  92.9 0.0 copy-done.31
  92.9 4.5 %update.1 = bf16[128,64,128]{2,1,0:T(8,128)(2,1)} custom-call(s32[1]{0:T(128)S(4)} %get-tuple-element.1155.live, f32[128]{0:T(128)S(1)} %get-tuple-element.1156.decay, bf16[128,64,128]{2,1,0:T(8,128)(2,1)} %get-tuple-element.1157.s, bf16[1,8192]{1,0:T(2,128)(2,1)S(1)} %copy-done, bf16[1,512]{1,0:T(2,128)(2,1)S(1)} %copy-done.31, ...), custom_call_target="tpu_custom_call" | custom-call | tf_op jit(solution)/shard_map/update/pallas_call | solution.py:270
  97.4 5.5 %all-to-all-done.1.parts = bf16[16,64,128]{2,1,0:T(8,128)(2,1)S(1)} async-done(((bf16[16,64,128]{2,1,0:T(8,128)(2,1)}), bf16[16,64,128]{2,1,0:T(8,128)(2,1)S(1)}, u32[]{:S(2)}, u32[]{:S(2)}) %all-to-all-start.1) | async-done | bytes 262176 | tf_op jit(solution)/shard_map/all_to_all | solution.py:292
  102.9 0.7 total.1
  (6 shorter events, 0.1 us)
Async XLA Ops:
  1.4 30.4 %collective-permute-start.23 = (bf16[1,128,64,128]{3,2,1,0:T(8,128)(2,1)}, bf16[1,128,64,128]{3,2,1,0:T(8,128)(2,1)}, u32[]{:S(2)}, u32[]{:S(2)}) collective-permute-start(bf16[1,128,64,128]{3,2,1,0:T(8,128)(2,1)} %get-tuple-element.875), channel_id=1, source_target_pairs={{4,2},{5,3},{6,0},{7,1},{12,10},{13,11},{14,8},{15,9},{20,18},{21,... | collective-permute-start | bytes 6291464 | tf_op jit(solution)/shard_map/cond/branch_11_fun/ppermute | solution.py:26
  3.6 10.7 %collective-permute-start.22 = (bf16[2,8960]{1,0:T(2,128)(2,1)S(1)}, bf16[2,8960]{1,0:T(2,128)(2,1)S(1)}, u32[]{:S(2)}, u32[]{:S(2)}) collective-permute-start(bf16[2,8960]{1,0:T(2,128)(2,1)S(1)} %pack.41), channel_id=1, source_target_pairs={{2,4},{3,5},{0,6},{1,7},{10,12},{11,13},{8,14},{9,15},{18,20},{19,... | collective-permute-start | bytes 107528 | tf_op jit(solution)/shard_map/cond/branch_11_fun/ppermute | solution.py:27
  11.5 2.8 %copy-start.43 = (f32[1,128]{1,0:T(1,128)S(1)}, f32[1,128]{1,0:T(1,128)}, u32[]{:S(2)}) copy-start(f32[1,128]{1,0:T(1,128)} %get-tuple-element.880.dt) | copy-start | bytes 1540 | tf_op jit(solution)/shard_map/cond
  11.5 2.8 %copy-start.73 = (f32[128]{0:T(128)S(1)}, f32[128]{0:T(128)}, u32[]{:S(2)}) copy-start(f32[128]{0:T(128)} %get-tuple-element.882) | copy-start | bytes 1540 | tf_op jit(solution)/shard_map/cond
  11.5 3.0 %copy-start.103 = (f32[128]{0:T(128)S(1)}, f32[128]{0:T(128)}, u32[]{:S(2)}) copy-start(f32[128]{0:T(128)} %get-tuple-element.883) | copy-start | bytes 1540 | tf_op jit(solution)/shard_map/cond
  11.5 5.0 %copy-start.12 = (f32[1,8192]{1,0:T(1,128)S(1)}, f32[1,8192]{1,0:T(1,128)}, u32[]{:S(2)}) copy-start(f32[1,8192]{1,0:T(1,128)} %get-tuple-element.884.gain) | copy-start | bytes 98308 | tf_op jit(solution)/shard_map/cond
  85.8 7.1 %copy-start = (bf16[1,8192]{1,0:T(2,128)(2,1)S(1)}, bf16[1,8192]{1,0:T(2,128)(2,1)}, u32[]{:S(2)}) copy-start(bf16[1,8192]{1,0:T(2,128)(2,1)} %x.1) | copy-start | bytes 49156
  85.8 7.2 %copy-start.31 = (bf16[1,512]{1,0:T(2,128)(2,1)S(1)}, bf16[1,512]{1,0:T(2,128)(2,1)}, u32[]{:S(2)}) copy-start(bf16[1,512]{1,0:T(2,128)(2,1)} %b.1) | copy-start | bytes 3076
  89.3 13.5 %all-to-all-start.1 = ((bf16[16,64,128]{2,1,0:T(8,128)(2,1)}), bf16[16,64,128]{2,1,0:T(8,128)(2,1)S(1)}, u32[]{:S(2)}, u32[]{:S(2)}) async-start(bf16[16,64,128]{2,1,0:T(8,128)(2,1)} %project.1), calls=%async_computation.1 | async-start | bytes 524288 | tf_op jit(solution)/shard_map/all_to_all | solution.py:292
